TPU v7x, 512 devices: a whole 4x8x8 slice. The times are simulated.
512 devices in a mesh: gx: 64 (over y, z), gy: 2 (over core), ma: 4 (over x).
Axes of the slice: x: 4, y: 8, z: 8, core: 2. Of those that a mesh axis runs over, the one named last changes fastest.
Arguments:
- ensemble: float32 [80, 2, 256, 256], P('ma', None, 'gx', 'gy'), may hold values from -6 to 6
- wind_field: float32 [2, 2, 256, 256], P(None, None, 'gx', 'gy'), may hold values from -0.45 to 0.45
- obs_value: float32 [4, 1024], replicated, may hold values from -6 to 6
- obs_var: float32 [4, 1024], replicated, may hold values from 2 to 20
- obs_region: int32 [4, 1024], replicated, may hold values from 0 to 127, as said below
- obs_cell: int32 [4, 1024], replicated, may hold values from 0 to 1023
- block_order: int32 [4], replicated, may hold values from 0 to 3, each once
- localization: float32 [64, 2, 4, 1024], P('gx', 'gy'), may hold values from 0 to 1
Outputs:
- analysis: float32 [80, 2, 256, 256], P('ma', None, 'gx', 'gy')
Inputs may be any that keep to these rules, and one draw needn't show every extreme that they name: `obs_region`: region index = first-dimension region * 2 + second-dimension region.
All inputs are finite; a program needn't handle non-finite values.
Results may differ from a plain program's by a relative error of at most 0.0001.
Values sent between devices are 32-bit elements; how exact they have to be, the bound alone decides.
No kernel may reach another device: no remote copies, remote signals or barrier semaphores. Data moves between devices by JAX's collectives and lax.ppermute only.
A program may use at most 64 MiB of HBM per device.

v0:
```python
import jax
import jax.numpy as jnp
from jax import lax
from jax.sharding import PartitionSpec as P

STEPS = 2
BLOCKS = 4
KAPPA = 0.025


def extended(block, sides, width):
    for axis, dim in sides:
        count = lax.axis_size(axis)
        forward = [(i, i + 1) for i in range(count - 1)]
        forward.append((count - 1, 0))
        backward = [(target, source) for source, target in forward]
        low = lax.ppermute(
            lax.slice_in_dim(block, block.shape[dim] - width, None, axis=dim), axis, forward
        )
        high = lax.ppermute(lax.slice_in_dim(block, 0, width, axis=dim), axis, backward)
        block = jnp.concatenate([low, block, high], axis=dim)
    return block


def advect(tracer, wind_field):
    padded = extended(tracer, (("gx", 2), ("gy", 3)), 1)
    east_wind = wind_field[0][None]
    north_wind = wind_field[1][None]
    middle = padded[:, :, 1:-1, 1:-1]
    west_side = padded[:, :, :-2, 1:-1]
    east_side = padded[:, :, 2:, 1:-1]
    south_side = padded[:, :, 1:-1, :-2]
    north_side = padded[:, :, 1:-1, 2:]
    return (
        middle
        - jnp.maximum(east_wind, 0.0) * (middle - west_side)
        - jnp.minimum(east_wind, 0.0) * (east_side - middle)
        - jnp.maximum(north_wind, 0.0) * (middle - south_side)
        - jnp.minimum(north_wind, 0.0) * (north_side - middle)
        + KAPPA * (east_side + west_side + north_side + south_side - 4.0 * middle)
    )


def mixing_matrix(prior_obs, observed, error_var, taper, ensemble_size):
    denom = ensemble_size - 1.0
    obs_mean = jnp.mean(prior_obs, axis=0)
    anomaly = prior_obs - obs_mean
    variance = jnp.sum(anomaly * anomaly, axis=0) / denom
    total_var = variance + error_var
    innovation = observed - obs_mean
    shrink = 1.0 / (1.0 + jnp.sqrt(error_var / total_var))
    gain_mean = taper * innovation / (denom * total_var)
    gain_spread = taper * shrink / (denom * total_var)
    shift_terms = jnp.dot(anomaly, gain_mean, precision=lax.Precision.HIGHEST)
    weighted = anomaly * gain_spread
    return shift_terms[:, None] - jnp.dot(weighted, anomaly.T, precision=lax.Precision.HIGHEST)


def local(
    ensemble, wind_field, obs_value, obs_var, obs_region, obs_cell, block_order, localization
):
    state = ensemble
    for step_index in range(STEPS):
        state = advect(state, wind_field)
    members_dev, levels, cells_x, cells_y = state.shape
    ensemble_size = members_dev * lax.axis_size("ma")
    own_region = lax.axis_index("gx") * lax.axis_size("gy") + lax.axis_index("gy")
    member_part = lax.axis_index("ma")
    stacked = state.reshape(members_dev, -1)
    for position in range(BLOCKS):
        block_id = block_order[position]
        gathered = lax.all_gather(stacked, "ma", axis=0, tiled=True)
        picked = jnp.take(gathered, obs_cell[block_id], axis=1)
        is_held = obs_region[block_id] == own_region
        prior_obs = lax.psum(jnp.where(is_held[None], picked, 0.0), ("gx", "gy"))
        mixing = mixing_matrix(
            prior_obs,
            obs_value[block_id],
            obs_var[block_id],
            localization[0, 0, block_id],
            ensemble_size,
        )
        center = jnp.mean(gathered, axis=0)
        own_columns = lax.dynamic_slice_in_dim(mixing, member_part * members_dev, members_dev, 1)
        stacked = stacked + jnp.dot(
            own_columns.T, gathered - center, precision=lax.Precision.HIGHEST
        )
    return stacked.reshape(state.shape)


def solution(mesh):
    in_specs = (
        P("ma", None, "gx", "gy"),
        P(None, None, "gx", "gy"),
        P(),
        P(),
        P(),
        P(),
        P(),
        P("gx", "gy", None, None),
    )
    out_specs = P("ma", None, "gx", "gy")
    return jax.shard_map(local, mesh=mesh, in_specs=in_specs, out_specs=out_specs, check_vma=False)
```

profile of v0, /device:TPU:24, one launch (start us, length us, event | category | flops | bytes accessed | tf_op | source)
XLA Modules:
  0.0 904.9 jit_solution(8745651643520247778)
XLA Ops:
  7.6 10.8 %collective-permute-start.1 = (f32[20,2,1,128]{3,2,1,0:T(1,128)S(1)}, f32[20,2,1,128]{3,2,1,0:T(1,128)S(1)}, u32[]{:S(2)}, u32[]{:S(2)}) collective-permute-start(f32[20,2,1,128]{3,2,1,0:T(1,128)S(1)} %get-tuple-element.29), channel_id=1, source_target_pairs={{8,0},{16,8},{24,16},{32,24},{40,32},{48,40},{56,48},{64,56},{72,6... | collective-permute-start | bytes 61448 | tf_op jit(solution)/shard_map/ppermute | solution.py:20
  18.4 2.1 collective-permute-start
  29.7 1.9 collective-permute-start.3
  31.7 2.4 collective-permute-start.2
  35.5 6.0 collective-permute-start.5
  41.6 1.9 collective-permute-start.4
  43.6 5.8 collective-permute-done.4
  49.5 1.9 collective-permute-start.7
  51.5 2.4 collective-permute-start.6
  55.4 12.9 %all-gather = f32[4,20,1024]{2,1,0:T(8,128)S(1)} all-gather(f32[1,20,1024]{2,1,0:T(8,128)S(1)} %reshape.117), channel_id=1, replica_groups=mesh['gx'=64,'gy'=2,'ma'=4] {'ma'}, dimensions={0}, use_global_device_ids=true | all-gather | bytes 409600 | tf_op jit(solution)/shard_map/all_gather | solution.py:72
  68.5 2.8 gather_fusion
  71.3 1.1 bitcast_select_fusion.3
  72.6 190.9 %all-reduce.5.cloned.1.call-done = f32[80,1024]{0,1:T(8,128)} async-done(((f32[80,1024]{0,1:T(8,128)}), f32[80,1024]{0,1:T(8,128)}) %all-reduce.5.cloned.1.call-update) | async-done | bytes 327696 | tf_op jit(solution)/shard_map/psum | solution.py:75
  263.5 1.3 reduce_sum.108
  265.6 1.5 fusion.6
  267.9 13.0 %all-gather.1 = f32[4,20,1024]{2,1,0:T(8,128)S(1)} all-gather(f32[1,20,1024]{2,1,0:T(8,128)S(1)} %bitcast.72), channel_id=1, replica_groups=mesh['gx'=64,'gy'=2,'ma'=4] {'ma'}, dimensions={0}, use_global_device_ids=true | all-gather | bytes 409600 | tf_op jit(solution)/shard_map/all_gather | solution.py:72
  281.1 2.8 gather_fusion.1
  283.9 1.1 bitcast_select_fusion.2
  285.2 188.6 %all-reduce.7.cloned.1.call-done = f32[80,1024]{0,1:T(8,128)} async-done(((f32[80,1024]{0,1:T(8,128)}), f32[80,1024]{0,1:T(8,128)}) %all-reduce.7.cloned.1.call-update) | async-done | bytes 327696 | tf_op jit(solution)/shard_map/psum | solution.py:75
  473.7 1.3 reduce_sum.111
  475.5 1.5 fusion.4
  477.8 13.0 %all-gather.2 = f32[4,20,1024]{2,1,0:T(8,128)S(1)} all-gather(f32[1,20,1024]{2,1,0:T(8,128)S(1)} %bitcast.73), channel_id=1, replica_groups=mesh['gx'=64,'gy'=2,'ma'=4] {'ma'}, dimensions={0}, use_global_device_ids=true | all-gather | bytes 409600 | tf_op jit(solution)/shard_map/all_gather | solution.py:72
  491.1 2.8 gather_fusion.2
  493.9 1.1 bitcast_select_fusion.1
  495.3 188.4 %all-reduce.9.cloned.1.call-done = f32[80,1024]{0,1:T(8,128)} async-done(((f32[80,1024]{0,1:T(8,128)}), f32[80,1024]{0,1:T(8,128)}) %all-reduce.9.cloned.1.call-update) | async-done | bytes 327696 | tf_op jit(solution)/shard_map/psum | solution.py:75
  683.7 1.3 reduce_sum.114
  685.5 1.5 fusion.2
  687.7 13.0 %all-gather.3 = f32[4,20,1024]{2,1,0:T(8,128)S(1)} all-gather(f32[1,20,1024]{2,1,0:T(8,128)S(1)} %bitcast.71), channel_id=1, replica_groups=mesh['gx'=64,'gy'=2,'ma'=4] {'ma'}, dimensions={0}, use_global_device_ids=true | all-gather | bytes 409600 | tf_op jit(solution)/shard_map/all_gather | solution.py:72
  701.0 2.8 gather_fusion.3
  705.0 188.6 %all-reduce.11.cloned.1.call-done = f32[80,1024]{0,1:T(8,128)} async-done(((f32[80,1024]{0,1:T(8,128)}), f32[80,1024]{0,1:T(8,128)}) %all-reduce.11.cloned.1.call-update) | async-done | bytes 327696 | tf_op jit(solution)/shard_map/psum | solution.py:75
  893.6 1.3 reduce_sum.117
  895.4 1.5 fusion
  (106 shorter events, 14.1 us)
Async XLA Ops:
  6.5 256.9 %all-reduce.5.cloned.1.call-start = ((), (), s32[]{:S(2)}) async-start(), calls=%async_computation | async-start | bytes 1048576 | tf_op jit(solution)/shard_map/psum | solution.py:75
  7.5 12.9 %copy-start.11 = (s32[4]{0:T(128)S(1)}, s32[4]{0:T(128)}, u32[]{:S(2)}) copy-start(s32[4]{0:T(128)} %param.16) | copy-start | bytes 52
  7.6 22.0 %collective-permute-start.1 = (f32[20,2,1,128]{3,2,1,0:T(1,128)S(1)}, f32[20,2,1,128]{3,2,1,0:T(1,128)S(1)}, u32[]{:S(2)}, u32[]{:S(2)}) collective-permute-start(f32[20,2,1,128]{3,2,1,0:T(1,128)S(1)} %get-tuple-element.29), channel_id=1, source_target_pairs={{8,0},{16,8},{24,16},{32,24},{40,32},{48,40},{56,48},{64,56},{72,6... | collective-permute-start | bytes 61448 | tf_op jit(solution)/shard_map/ppermute | solution.py:20
  18.4 10.4 %copy-start.7 = (s32[4,1024]{1,0:T(4,128)S(1)}, s32[4,1024]{1,0:T(4,128)}, u32[]{:S(2)}) copy-start(s32[4,1024]{1,0:T(4,128)} %param.15) | copy-start | bytes 49156
  18.4 11.1 %copy-start.4 = (f32[20,2,4,128]{3,2,1,0:T(4,128)S(1)}, f32[20,2,4,128]{3,2,1,0:T(4,128)}, u32[]{:S(2)}) copy-start(f32[20,2,4,128]{3,2,1,0:T(4,128)} %param.10) | copy-start | bytes 245764
  18.4 11.1 %collective-permute-start = (f32[20,2,1,128]{3,2,1,0:T(1,128)S(1)}, f32[20,2,1,128]{3,2,1,0:T(1,128)S(1)}, u32[]{:S(2)}, u32[]{:S(2)}) collective-permute-start(f32[20,2,1,128]{3,2,1,0:T(1,128)S(1)} %get-tuple-element.28), channel_id=1, source_target_pairs={{0,8},{8,16},{16,24},{24,32},{32,40},{40,48},{48,56},{56,64},{64,7... | collective-permute-start | bytes 61448 | tf_op jit(solution)/shard_map/ppermute | solution.py:17
  28.8 0.7 copy-start.10
  29.7 4.4 collective-permute-start.3
  31.7 3.4 collective-permute-start.2
  35.5 8.0 copy-start.8
  35.5 8.0 collective-permute-start.5
  41.6 7.8 collective-permute-start.4
  49.4 4.5 copy-start.9
  49.5 4.4 collective-permute-start.7
  51.5 3.4 collective-permute-start.6
  72.5 401.2 %all-reduce.7.cloned.1.call-start = ((), (), s32[]{:S(2)}) async-start(), calls=%async_computation.1 | async-start | bytes 1048576 | tf_op jit(solution)/shard_map/psum | solution.py:75
  263.5 1.3 copy-start
  264.8 0.7 copy-start.5
  264.8 0.7 copy-start.6
  285.1 398.6 %all-reduce.9.cloned.1.call-start = ((), (), s32[]{:S(2)}) async-start(), calls=%async_computation.2 | async-start | bytes 1048576 | tf_op jit(solution)/shard_map/psum | solution.py:75
  473.7 1.3 copy-start.1
  495.0 398.6 %all-reduce.11.cloned.1.call-start = ((), (), s32[]{:S(2)}) async-start(), calls=%async_computation.3 | async-start | bytes 1048576 | tf_op jit(solution)/shard_map/psum | solution.py:75
  683.7 1.3 copy-start.2
  893.6 1.3 copy-start.3
Sparse Core Ops, SparseCore 0:
  72.6 190.7 all-reduce.4
  285.2 188.4 all-reduce.6
  495.2 188.4 all-reduce.8
  705.1 188.4 all-reduce.10
where the time goes:
time: 906 us; the launch traced here: 905 us
  waiting for transfers between devices  764 us (84%)
  blocking collectives  51.8 us (6%)
  starting transfers between devices  29.8 us (3%)
  between operations  21.4 us (2%)
  local copies, waits for them, and re-layouts  15.9 us (2%)
  other arithmetic  12.7 us (1%)
    psum x4, waiting for transfers between devices, local(): prior_obs = lax.psum(jnp.where(is_held[None], picked, 0.0), ('gx', 'gy'))  756 us
    all_gather x4, blocking collectives, local(): gathered = lax.all_gather(stacked, 'ma', axis=0, tiled=True)  51.8 us
    ppermute x4, starting transfers between devices, extended(): lax.ppermute(lax.slice_in_dim(block, 0, width, axis=dim), axis, backward)  20.7 us
  transfers between devices with their start and end apart: 12, of which 7 were waited for; matrix products, arithmetic and copies ran while one was open for 0% of the time, Pallas kernels for 0%

commit v1 on v0

--- a/solution.py
+++ b/solution.py
@@ -72,7 +72,8 @@
         gathered = lax.all_gather(stacked, "ma", axis=0, tiled=True)
         picked = jnp.take(gathered, obs_cell[block_id], axis=1)
         is_held = obs_region[block_id] == own_region
-        prior_obs = lax.psum(jnp.where(is_held[None], picked, 0.0), ("gx", "gy"))
+        partial = lax.psum(jnp.where(is_held[None], picked, 0.0), "gx")
+        prior_obs = lax.psum(partial, "gy")
         mixing = mixing_matrix(
             prior_obs,
             obs_value[block_id],

time: 906 us -> 915 us (level)
  the two profiles are of different devices: /device:TPU:24 before, /device:TPU:1 now
where the time goes in v1:
time: 915 us; the launch traced here: 914 us
  waiting for transfers between devices  779 us (85%)
  blocking collectives  39.4 us (4%)
  starting transfers between devices  35.9 us (4%)
  between operations  21.8 us (2%)
  local copies, waits for them, and re-layouts  15.9 us (2%)
  other arithmetic  12.7 us (1%)
    psum x4, waiting for transfers between devices, local(): partial = lax.psum(jnp.where(is_held[None], picked, 0.0), 'gx')  611 us
    psum x4, waiting for transfers between devices, local(): prior_obs = lax.psum(partial, 'gy')  160 us
    all_gather x4, blocking collectives, local(): gathered = lax.all_gather(stacked, 'ma', axis=0, tiled=True)  39.4 us
    ppermute x4, starting transfers between devices, extended(): lax.ppermute(lax.slice_in_dim(block, 0, width, axis=dim), axis, backward)  27.7 us
  transfers between devices with their start and end apart: 16, of which 11 were waited for; matrix products, arithmetic and copies ran while one was open for 0% of the time, Pallas kernels for 0%

profile of v1, /device:TPU:1, one launch (start us, length us, event | category | flops | bytes accessed | tf_op | source)
XLA Modules:
  0.0 914.2 jit_solution(16888553405415975835)
XLA Ops:
  7.6 14.4 %collective-permute-start.1 = (f32[20,2,1,128]{3,2,1,0:T(1,128)S(1)}, f32[20,2,1,128]{3,2,1,0:T(1,128)S(1)}, u32[]{:S(2)}, u32[]{:S(2)}) collective-permute-start(f32[20,2,1,128]{3,2,1,0:T(1,128)S(1)} %get-tuple-element.29), channel_id=1, source_target_pairs={{8,0},{16,8},{24,16},{32,24},{40,32},{48,40},{56,48},{64,56},{72,6... | collective-permute-start | bytes 61448 | tf_op jit(solution)/shard_map/ppermute | solution.py:20
  22.0 1.9 collective-permute-start
  32.5 2.9 collective-permute-start.3
  35.4 1.9 collective-permute-start.2
  37.4 1.3 collective-permute-done.2
  39.1 7.0 collective-permute-start.5
  46.1 1.9 collective-permute-start.4
  48.1 5.9 collective-permute-done.4
  54.1 3.5 collective-permute-start.7
  57.6 1.9 collective-permute-start.6
  61.3 10.5 %all-gather = f32[4,20,1024]{2,1,0:T(8,128)S(1)} all-gather(f32[1,20,1024]{2,1,0:T(8,128)S(1)} %reshape.117), channel_id=1, replica_groups=mesh['gx'=64,'gy'=2,'ma'=4] {'ma'}, dimensions={0}, use_global_device_ids=true | all-gather | bytes 409600 | tf_op jit(solution)/shard_map/all_gather | solution.py:72
  72.1 2.8 gather_fusion
  76.2 146.6 %all-reduce.9.cloned.1.call-done = f32[80,1024]{0,1:T(8,128)} async-done(((f32[80,1024]{0,1:T(8,128)}), f32[80,1024]{0,1:T(8,128)}) %all-reduce.9.cloned.1.call-update) | async-done | bytes 327696 | tf_op jit(solution)/shard_map/psum | solution.py:75
  223.6 39.6 %all-reduce.11.cloned.1.call-done = f32[80,1024]{0,1:T(8,128)} async-done(((f32[80,1024]{0,1:T(8,128)}), f32[80,1024]{0,1:T(8,128)}) %all-reduce.11.cloned.1.call-update) | async-done | bytes 327696 | tf_op jit(solution)/shard_map/psum | solution.py:76
  263.1 1.3 reduce_sum.108
  265.3 1.5 fusion.6
  267.5 9.6 %all-gather.1 = f32[4,20,1024]{2,1,0:T(8,128)S(1)} all-gather(f32[1,20,1024]{2,1,0:T(8,128)S(1)} %bitcast.71), channel_id=1, replica_groups=mesh['gx'=64,'gy'=2,'ma'=4] {'ma'}, dimensions={0}, use_global_device_ids=true | all-gather | bytes 409600 | tf_op jit(solution)/shard_map/all_gather | solution.py:72
  277.4 2.8 gather_fusion.1
  281.5 154.7 %all-reduce.13.cloned.1.call-done = f32[80,1024]{0,1:T(8,128)} async-done(((f32[80,1024]{0,1:T(8,128)}), f32[80,1024]{0,1:T(8,128)}) %all-reduce.13.cloned.1.call-update) | async-done | bytes 327696 | tf_op jit(solution)/shard_map/psum | solution.py:75
  436.4 40.1 %all-reduce.15.cloned.1.call-done = f32[80,1024]{0,1:T(8,128)} async-done(((f32[80,1024]{0,1:T(8,128)}), f32[80,1024]{0,1:T(8,128)}) %all-reduce.15.cloned.1.call-update) | async-done | bytes 327696 | tf_op jit(solution)/shard_map/psum | solution.py:76
  476.5 1.3 reduce_sum.111
  478.3 1.5 fusion.4
  480.5 9.6 %all-gather.2 = f32[4,20,1024]{2,1,0:T(8,128)S(1)} all-gather(f32[1,20,1024]{2,1,0:T(8,128)S(1)} %bitcast.73), channel_id=1, replica_groups=mesh['gx'=64,'gy'=2,'ma'=4] {'ma'}, dimensions={0}, use_global_device_ids=true | all-gather | bytes 409600 | tf_op jit(solution)/shard_map/all_gather | solution.py:72
  490.4 2.8 gather_fusion.2
  494.5 154.8 %all-reduce.17.cloned.1.call-done = f32[80,1024]{0,1:T(8,128)} async-done(((f32[80,1024]{0,1:T(8,128)}), f32[80,1024]{0,1:T(8,128)}) %all-reduce.17.cloned.1.call-update) | async-done | bytes 327696 | tf_op jit(solution)/shard_map/psum | solution.py:75
  649.5 39.9 %all-reduce.19.cloned.1.call-done = f32[80,1024]{0,1:T(8,128)} async-done(((f32[80,1024]{0,1:T(8,128)}), f32[80,1024]{0,1:T(8,128)}) %all-reduce.19.cloned.1.call-update) | async-done | bytes 327696 | tf_op jit(solution)/shard_map/psum | solution.py:76
  691.3 1.5 fusion.2
  693.5 9.6 %all-gather.3 = f32[4,20,1024]{2,1,0:T(8,128)S(1)} all-gather(f32[1,20,1024]{2,1,0:T(8,128)S(1)} %bitcast.72), channel_id=1, replica_groups=mesh['gx'=64,'gy'=2,'ma'=4] {'ma'}, dimensions={0}, use_global_device_ids=true | all-gather | bytes 409600 | tf_op jit(solution)/shard_map/all_gather | solution.py:72
  703.4 2.8 gather_fusion.3
  707.5 154.8 %all-reduce.21.cloned.1.call-done = f32[80,1024]{0,1:T(8,128)} async-done(((f32[80,1024]{0,1:T(8,128)}), f32[80,1024]{0,1:T(8,128)}) %all-reduce.21.cloned.1.call-update) | async-done | bytes 327696 | tf_op jit(solution)/shard_map/psum | solution.py:75
  862.3 40.3 %all-reduce.23.cloned.1.call-done = f32[80,1024]{0,1:T(8,128)} async-done(((f32[80,1024]{0,1:T(8,128)}), f32[80,1024]{0,1:T(8,128)}) %all-reduce.23.cloned.1.call-update) | async-done | bytes 327696 | tf_op jit(solution)/shard_map/psum | solution.py:76
  904.4 1.5 fusion
  (118 shorter events, 19.8 us)
Async XLA Ops:
  6.5 25.8 %copy-start.4 = (f32[20,2,4,128]{3,2,1,0:T(4,128)S(1)}, f32[20,2,4,128]{3,2,1,0:T(4,128)}, u32[]{:S(2)}) copy-start(f32[20,2,4,128]{3,2,1,0:T(4,128)} %param.10) | copy-start | bytes 245764
  6.5 216.2 %all-reduce.9.cloned.1.call-start = ((), (), s32[]{:S(2)}) async-start(), calls=%async_computation | async-start | bytes 1048576 | tf_op jit(solution)/shard_map/psum | solution.py:75
  7.6 16.4 %copy-start.11 = (s32[4]{0:T(128)S(1)}, s32[4]{0:T(128)}, u32[]{:S(2)}) copy-start(s32[4]{0:T(128)} %param.16) | copy-start | bytes 52
  7.6 24.7 %collective-permute-start.1 = (f32[20,2,1,128]{3,2,1,0:T(1,128)S(1)}, f32[20,2,1,128]{3,2,1,0:T(1,128)S(1)}, u32[]{:S(2)}, u32[]{:S(2)}) collective-permute-start(f32[20,2,1,128]{3,2,1,0:T(1,128)S(1)} %get-tuple-element.29), channel_id=1, source_target_pairs={{8,0},{16,8},{24,16},{32,24},{40,32},{48,40},{56,48},{64,56},{72,6... | collective-permute-start | bytes 61448 | tf_op jit(solution)/shard_map/ppermute | solution.py:20
  22.0 10.3 %collective-permute-start = (f32[20,2,1,128]{3,2,1,0:T(1,128)S(1)}, f32[20,2,1,128]{3,2,1,0:T(1,128)S(1)}, u32[]{:S(2)}, u32[]{:S(2)}) collective-permute-start(f32[20,2,1,128]{3,2,1,0:T(1,128)S(1)} %get-tuple-element.28), channel_id=1, source_target_pairs={{0,8},{8,16},{16,24},{24,32},{32,40},{40,48},{48,56},{56,64},{64,7... | collective-permute-start | bytes 61448 | tf_op jit(solution)/shard_map/ppermute | solution.py:17
  27.3 2.4 copy-start.10
  29.7 2.6 copy-start.7
  32.5 4.8 collective-permute-start.3
  35.4 3.3 collective-permute-start.2
  39.1 8.9 collective-permute-start.5
  46.1 7.8 collective-permute-start.4
  54.0 5.6 copy-start.8
  54.1 5.5 collective-permute-start.7
  57.6 3.3 collective-permute-start.6
  76.1 187.0 %all-reduce.11.cloned.1.call-start = ((), (), s32[]{:S(2)}) async-start(), calls=%async_computation.1 | async-start | bytes 1048576 | tf_op jit(solution)/shard_map/psum | solution.py:76
  222.7 0.7 copy-start.9
  222.7 213.5 %all-reduce.13.cloned.1.call-start = ((), (), s32[]{:S(2)}) async-start(), calls=%async_computation.2 | async-start | bytes 1048576 | tf_op jit(solution)/shard_map/psum | solution.py:75
  263.1 1.3 copy-start
  264.5 0.7 copy-start.5
  264.5 0.7 copy-start.6
  281.4 195.1 %all-reduce.15.cloned.1.call-start = ((), (), s32[]{:S(2)}) async-start(), calls=%async_computation.3 | async-start | bytes 1048576 | tf_op jit(solution)/shard_map/psum | solution.py:76
  436.2 213.0 %all-reduce.17.cloned.1.call-start = ((), (), s32[]{:S(2)}) async-start(), calls=%async_computation.4 | async-start | bytes 1048576 | tf_op jit(solution)/shard_map/psum | solution.py:75
  476.5 1.3 copy-start.1
  494.4 195.1 %all-reduce.19.cloned.1.call-start = ((), (), s32[]{:S(2)}) async-start(), calls=%async_computation.5 | async-start | bytes 1048576 | tf_op jit(solution)/shard_map/psum | solution.py:76
  649.2 213.0 %all-reduce.21.cloned.1.call-start = ((), (), s32[]{:S(2)}) async-start(), calls=%async_computation.6 | async-start | bytes 1048576 | tf_op jit(solution)/shard_map/psum | solution.py:75
  689.5 1.3 copy-start.2
  707.4 195.2 %all-reduce.23.cloned.1.call-start = ((), (), s32[]{:S(2)}) async-start(), calls=%async_computation.7 | async-start | bytes 1048576 | tf_op jit(solution)/shard_map/psum | solution.py:76
  902.6 1.3 copy-start.3
Sparse Core Ops, SparseCore 0:
  76.2 146.4 all-reduce.8
  225.9 37.2 all-reduce.10
  281.5 154.6 all-reduce.12
  439.2 37.2 all-reduce.14
  494.5 154.6 all-reduce.16
  652.2 37.2 all-reduce.18
  707.5 154.6 all-reduce.20
  865.4 37.2 all-reduce.22
